TPU v7x, 512 devices: a whole 4x4x16 slice. The times are simulated.
512 devices in a mesh: slab: 32 (over x, y, z_hi), tile: 16 (over z_lo, core).
Axes of the slice: x: 4, y: 4, z: 16 (z_hi: 2, z_lo: 8; z = z_hi * 8 + z_lo), core: 2. Of those that a mesh axis runs over, the one named last changes fastest.
Arguments:
- field: float32 [256, 256, 1024], P('slab', 'tile'), may hold values from -1 to 1
- dual: float32 [3, 256, 256, 1024], P(None, 'slab', 'tile'), may hold values from -0.5 to 0.5
- depth: float32 [32, 2, 4, 256, 1024], P('slab', None, None, 'tile'), may hold values from 0 to 256
- owner: int32 [2], replicated, may hold values from 0 to 31
- visible: int32 [2, 4, 16], P(None, None, 'tile'), may hold values 0 or 1
Outputs:
- field_out: float32 [256, 256, 1024], P('slab', 'tile')
- dual_out: float32 [3, 256, 256, 1024], P(None, 'slab', 'tile')
All inputs are finite; a program needn't handle non-finite values. No bound on the sum of `visible` on one device may be relied on, other than what follows from the above.
Results may differ from a plain program's by a relative error of at most 0.00002.
Values sent between devices are 32-bit elements; how exact they have to be, the bound alone decides.
No kernel may reach another device: no remote copies, remote signals or barrier semaphores. Data moves between devices by JAX's collectives and lax.ppermute only.
A program may use at most 64 MiB of HBM per device.

v0:
```python
import jax
import jax.numpy as jnp
from jax import lax
from jax.sharding import PartitionSpec as P

VIEWS = 4
BINS = 8
BAND = 6
ITERS = 2


def from_root(value, axis, root):
    mine = lax.axis_index(axis) == root
    return lax.psum(jnp.where(mine, value, jnp.zeros_like(value)), axis)


def passed_along(value, axis, steps):
    count = lax.axis_size(axis)
    first, last = (max(0, -steps), min(count, count - steps))
    return lax.ppermute(value, axis, [(source, source + steps) for source in range(first, last)])


def add_votes(histogram, depth_map, seen, zfloat):
    ratio = (depth_map[None, :, :] - zfloat) / float(BAND)
    weight = jnp.clip(ratio + 2.0, 0.0, 1.0) * seen
    place = (jnp.clip(ratio, -1.0, 1.0) + 1.0) * ((BINS - 1) / 2.0)
    return [
        histogram[bin_index] + weight * jnp.maximum(0.0, 1.0 - jnp.abs(place - float(bin_index)))
        for bin_index in range(BINS)
    ]


def proximal(values, histogram):
    total = histogram[0]
    for bin_index in range(1, BINS):
        total = total + histogram[bin_index]
    weights = -total
    best = jnp.minimum(values - 0.05 * weights, -1.0)
    weights = weights + 2.0 * histogram[0]
    for bin_index in range(1, BINS):
        centre = -1.0 + 2.0 * bin_index / (BINS - 1)
        best = jnp.maximum(best, jnp.minimum(values - 0.05 * weights, centre))
        weights = weights + 2.0 * histogram[bin_index]
    return jnp.maximum(best, values - 0.05 * weights)


def dual_step(
    dual_z, dual_x, dual_y, here, ahead_z, ahead_x, zpos, xpos, ypos, total_z, total_x, total_y
):
    zero_y = jnp.zeros(here.shape[:2] + (1,), jnp.float32)
    ahead_y = jnp.concatenate([here[:, :, 1:], zero_y], 2)
    grad_z = jnp.where(zpos < total_z - 1, ahead_z - here, 0.0)
    grad_x = jnp.where(xpos < total_x - 1, ahead_x - here, 0.0)
    grad_y = jnp.where(ypos < total_y - 1, ahead_y - here, 0.0)
    moved_z = dual_z + 0.25 * grad_z
    moved_x = dual_x + 0.25 * grad_x
    moved_y = dual_y + 0.25 * grad_y
    scale = jnp.maximum(1.0, jnp.sqrt(moved_z * moved_z + moved_x * moved_x + moved_y * moved_y))
    inside_z = (zpos >= 0) & (zpos < total_z - 1)
    inside_x = (xpos >= 0) & (xpos < total_x - 1)
    new_z = jnp.where(inside_z, moved_z / scale, 0.0)
    new_x = jnp.where(inside_x, moved_x / scale, 0.0)
    new_y = jnp.where(ypos < total_y - 1, moved_y / scale, 0.0)
    return (new_z, new_x, new_y)


def per_device(field, dual, depth, owner, visible):
    slab_cells, strip_cells, depth_cells = field.shape
    total_z = slab_cells * lax.axis_size("slab")
    total_x = strip_cells * lax.axis_size("tile")
    slab_start = lax.axis_index("slab") * slab_cells
    strip_start = lax.axis_index("tile") * strip_cells
    zpos = slab_start + jnp.arange(slab_cells, dtype=jnp.int32)[:, None, None]
    xpos = strip_start + jnp.arange(strip_cells, dtype=jnp.int32)[None, :, None]
    ypos = jnp.arange(depth_cells, dtype=jnp.int32)[None, None, :]
    zfloat = zpos.astype(jnp.float32)
    histogram = [jnp.zeros(field.shape, jnp.float32) for bin_index in range(BINS)]
    current = field
    dual_z, dual_x, dual_y = (dual[0], dual[1], dual[2])
    extra = field
    zero_y = jnp.zeros((slab_cells, strip_cells, 1), jnp.float32)
    for step_index in range(ITERS):
        batch = from_root(depth[0, step_index], "slab", owner[step_index])
        for view_index in range(VIEWS):
            seen = visible[step_index, view_index, 0].astype(jnp.float32)
            histogram = add_votes(histogram, batch[view_index], seen, zfloat)
        below = passed_along(extra[0:1], "slab", -1)
        beside = passed_along(extra[:, 0:1], "tile", -1)
        ahead_z = jnp.concatenate([extra[1:], below], 0)
        ahead_x = jnp.concatenate([extra[:, 1:], beside], 1)
        dual_z, dual_x, dual_y = dual_step(
            dual_z,
            dual_x,
            dual_y,
            extra,
            ahead_z,
            ahead_x,
            zpos,
            xpos,
            ypos,
            total_z,
            total_x,
            depth_cells,
        )
        above = passed_along(dual_z[-1:], "slab", 1)
        before = passed_along(dual_x[:, -1:], "tile", 1)
        prev_z = jnp.concatenate([above, dual_z[:-1]], 0)
        prev_x = jnp.concatenate([before, dual_x[:, :-1]], 1)
        prev_y = jnp.concatenate([zero_y, dual_y[:, :, :-1]], 2)
        divergence = dual_z - prev_z + (dual_x - prev_x) + (dual_y - prev_y)
        updated = proximal(current + 0.25 * divergence, histogram)
        extra = 2.0 * updated - current
        current = updated
    return (current, jnp.stack([dual_z, dual_x, dual_y]))


def solution(mesh):
    placed = (
        P("slab", "tile", None),
        P(None, "slab", "tile", None),
        P("slab", None, None, "tile", None),
        P(),
        P(None, None, "tile"),
    )
    return jax.shard_map(
        per_device,
        mesh=mesh,
        in_specs=placed,
        out_specs=(P("slab", "tile", None), P(None, "slab", "tile", None)),
        check_vma=False,
    )
```

profile of v0, /device:TPU:23, one launch (start us, length us, event | category | flops | bytes accessed | tf_op | source)
XLA Modules:
  0.0 672.6 jit_solution(14026309236746614929)
XLA Ops:
  7.2 0.0 copy-start
  7.2 0.0 copy-start.2
  7.2 0.0 all-reduce.7.cloned.1.call-start
  7.2 1.0 slice.134
  8.3 2.6 collective-permute-start.1
  10.8 0.8 slice.131
  11.7 15.3 %collective-permute-start = (f32[1,16,1024]{2,1,0:T(8,128)S(1)}, f32[1,16,1024]{2,1,0:T(8,128)S(1)}, u32[]{:S(2)}, u32[]{:S(2)}) collective-permute-start(f32[1,16,1024]{2,1,0:T(8,128)S(1)} %slice.131), channel_id=1, source_target_pairs={{16,0},{32,16},{48,32},{64,48},{80,64},{96,80},{112,96},{128,112},... | collective-permute-start | bytes 196616 | tf_op jit(solution)/shard_map/ppermute | solution.py:20
  27.0 1.3 fusion.28
  29.6 1.9 select_bitcast_fusion
  31.5 0.0 all-reduce.7.cloned.1.call-update
  31.5 0.0 slice-start
  31.6 0.0 copy-done.2
  31.6 0.7 fusion.27
  32.3 0.0 copy-done
  32.3 0.1 slice.133
  32.3 0.2 slice.136
  37.4 0.0 collective-permute-done.1
  37.4 0.0 collective-permute-done
  37.5 0.0 slice-done
  37.5 2.0 divide_select_fusion.3
  39.4 0.3 divide_select_fusion.5
  39.9 3.3 collective-permute-start.3
  43.1 9.4 %collective-permute-start.2 = (f32[1,16,1024]{2,1,0:T(8,128)S(1)}, f32[1,16,1024]{2,1,0:T(8,128)S(1)}, u32[]{:S(2)}, u32[]{:S(2)}) collective-permute-start(f32[1,16,1024]{2,1,0:T(8,128)S(1)} %slice.172), channel_id=1, source_target_pairs={{0,16},{16,32},{32,48},{48,64},{64,80},{80,96},{96,112},{112,128},... | collective-permute-start | bytes 196616 | tf_op jit(solution)/shard_map/ppermute | solution.py:20
  52.5 534.5 %all-reduce.7.cloned.1.call-done = (f32[4,16,1024]{2,1,0:T(8,128)}, f32[4,16,1024]{2,1,0:T(8,128)}) async-done(((f32[4,16,1024]{2,1,0:T(8,128)}, f32[4,16,1024]{2,1,0:T(8,128)}), (f32[4,16,1024]{2,1,0:T(8,128)}, f32[4,16,1024]{2,1,0:T(8,128)})) %all-reduce.7.cloned.1.call-update) | async-done | bytes 524304 | tf_op jit(solution)/shard_map/psum | solution.py:14
  587.0 1.0 slice_bitcast_fusion.7
  588.0 0.0 collective-permute-done.3
  588.0 0.0 collective-permute-done.2
  588.0 0.0 copy-start.1
  588.0 5.0 multiply_subtract_fusion
  593.1 24.7 %collective-permute-start.5 = (f32[8,1,1024]{2,1,0:T(1,128)S(1)}, f32[8,1,1024]{2,1,0:T(1,128)S(1)}, u32[]{:S(2)}, u32[]{:S(2)}) collective-permute-start(f32[8,1,1024]{2,1,0:T(1,128)S(1)} %slice.184), channel_id=1, source_target_pairs={{1,0},{2,1},{3,2},{4,3},{5,4},{6,5},{7,6},{8,7},{9,8},{10,9},{11,1... | collective-permute-start | bytes 98312 | tf_op jit(solution)/shard_map/ppermute | solution.py:20
  617.8 2.4 collective-permute-start.4
  620.2 0.0 copy-done.1
  620.3 0.2 slice.185
  620.5 0.1 slice.183
  620.5 0.0 collective-permute-done.5
  620.6 12.3 %collective-permute-done.4 = f32[1,16,1024]{2,1,0:T(8,128)S(1)} collective-permute-done((f32[1,16,1024]{2,1,0:T(8,128)S(1)}, f32[1,16,1024]{2,1,0:T(8,128)S(1)}, u32[]{:S(2)}, u32[]{:S(2)}) %collective-permute-start.4) | collective-permute-done | bytes 65568 | tf_op jit(solution)/shard_map/ppermute | solution.py:20
  632.9 0.6 divide_select_fusion
  633.4 0.2 divide_select_fusion.2
  633.7 3.1 collective-permute-start.7
  636.8 10.0 %collective-permute-start.6 = (f32[1,16,1024]{2,1,0:T(8,128)S(1)}, f32[1,16,1024]{2,1,0:T(8,128)S(1)}, u32[]{:S(2)}, u32[]{:S(2)}) collective-permute-start(f32[1,16,1024]{2,1,0:T(8,128)S(1)} %slice.186), channel_id=1, source_target_pairs={{0,16},{16,32},{32,48},{48,64},{64,80},{80,96},{96,112},{112,128},... | collective-permute-start | bytes 196616 | tf_op jit(solution)/shard_map/ppermute | solution.py:20
  646.8 1.2 pad_maximum_fusion
  648.1 0.0 collective-permute-done.7
  648.1 8.1 %collective-permute-done.6 = f32[1,16,1024]{2,1,0:T(8,128)S(1)} collective-permute-done((f32[1,16,1024]{2,1,0:T(8,128)S(1)}, f32[1,16,1024]{2,1,0:T(8,128)S(1)}, u32[]{:S(2)}, u32[]{:S(2)}) %collective-permute-start.6) | collective-permute-done | bytes 65568 | tf_op jit(solution)/shard_map/ppermute | solution.py:20
  656.2 9.6 %subtract_maximum_fusion = f32[8,16,1024]{2,1,0:T(8,128)} fusion(f32[8,16,1024]{2,1,0:T(8,128)S(1)} %get-tuple-element.9, f32[8,16,1024]{2,1,0:T(8,128)S(1)} %get-tuple-element.17, f32[8,15,1024]{2,1,0:T(8,128)S(1)} %bitcast.48, f32[8,1,1024]{2,1,0:T(1,128)S(1)} %collective-permute-done.7, f32[8,16,1024]{2,1,0:T(8,128)S(1)} %get-tuple-element.16, ...), kind=kLoop, calls=%fused_computation.30 | loop fusion | flops 65404928 | bytes 4718144 | tf_op jit(solution)/shard_map/max | solution.py:44
  (14 shorter events, 0.2 us)
Async XLA Ops:
  7.2 25.1 %copy-start = (f32[8,16,1024]{2,1,0:T(8,128)S(1)}, f32[8,16,1024]{2,1,0:T(8,128)}, u32[]{:S(2)}) copy-start(f32[8,16,1024]{2,1,0:T(8,128)} %param.5) | copy-start | bytes 1572868
  7.2 24.4 %copy-start.2 = (s32[2,4,1]{1,2,0:T(1,128)S(1)}, s32[2,4,1]{1,2,0:T(1,128)}, u32[]{:S(2)}) copy-start(s32[2,4,1]{1,2,0:T(1,128)} %param.9) | copy-start | bytes 100
  7.2 579.8 %all-reduce.7.cloned.1.call-start = ((), (), s32[]{:S(2)}) async-start(), calls=%async_computation | async-start | bytes 1048576 | tf_op jit(solution)/shard_map/psum | solution.py:14
  8.3 29.2 %collective-permute-start.1 = (f32[8,1,1024]{2,1,0:T(1,128)S(1)}, f32[8,1,1024]{2,1,0:T(1,128)S(1)}, u32[]{:S(2)}, u32[]{:S(2)}) collective-permute-start(f32[8,1,1024]{2,1,0:T(1,128)S(1)} %slice.134), channel_id=1, source_target_pairs={{1,0},{2,1},{3,2},{4,3},{5,4},{6,5},{7,6},{8,7},{9,8},{10,9},{11,1... | collective-permute-start | bytes 98312 | tf_op jit(solution)/shard_map/ppermute | solution.py:20
  11.7 25.8 %collective-permute-start = (f32[1,16,1024]{2,1,0:T(8,128)S(1)}, f32[1,16,1024]{2,1,0:T(8,128)S(1)}, u32[]{:S(2)}, u32[]{:S(2)}) collective-permute-start(f32[1,16,1024]{2,1,0:T(8,128)S(1)} %slice.131), channel_id=1, source_target_pairs={{16,0},{32,16},{48,32},{64,48},{80,64},{96,80},{112,96},{128,112},... | collective-permute-start | bytes 196616 | tf_op jit(solution)/shard_map/ppermute | solution.py:20
  31.5 5.9 slice-start
  39.9 548.1 %collective-permute-start.3 = (f32[8,1,1024]{2,1,0:T(1,128)S(1)}, f32[8,1,1024]{2,1,0:T(1,128)S(1)}, u32[]{:S(2)}, u32[]{:S(2)}) collective-permute-start(f32[8,1,1024]{2,1,0:T(1,128)S(1)} %slice.174), channel_id=1, source_target_pairs={{0,1},{1,2},{2,3},{3,4},{4,5},{5,6},{6,7},{7,8},{8,9},{9,10},{10,1... | collective-permute-start | bytes 98312 | tf_op jit(solution)/shard_map/ppermute | solution.py:20
  43.1 544.8 %collective-permute-start.2 = (f32[1,16,1024]{2,1,0:T(8,128)S(1)}, f32[1,16,1024]{2,1,0:T(8,128)S(1)}, u32[]{:S(2)}, u32[]{:S(2)}) collective-permute-start(f32[1,16,1024]{2,1,0:T(8,128)S(1)} %slice.172), channel_id=1, source_target_pairs={{0,16},{16,32},{32,48},{48,64},{64,80},{80,96},{96,112},{112,128},... | collective-permute-start | bytes 196616 | tf_op jit(solution)/shard_map/ppermute | solution.py:20
  588.0 32.2 %copy-start.1 = (f32[4,16,1024]{2,1,0:T(8,128)S(1)}, f32[4,16,1024]{2,1,0:T(8,128)}, u32[]{:S(2)}) copy-start(f32[4,16,1024]{2,1,0:T(8,128)} %get-tuple-element.3) | copy-start | bytes 786436
  593.1 27.5 %collective-permute-start.5 = (f32[8,1,1024]{2,1,0:T(1,128)S(1)}, f32[8,1,1024]{2,1,0:T(1,128)S(1)}, u32[]{:S(2)}, u32[]{:S(2)}) collective-permute-start(f32[8,1,1024]{2,1,0:T(1,128)S(1)} %slice.184), channel_id=1, source_target_pairs={{1,0},{2,1},{3,2},{4,3},{5,4},{6,5},{7,6},{8,7},{9,8},{10,9},{11,1... | collective-permute-start | bytes 98312 | tf_op jit(solution)/shard_map/ppermute | solution.py:20
  617.8 15.1 %collective-permute-start.4 = (f32[1,16,1024]{2,1,0:T(8,128)S(1)}, f32[1,16,1024]{2,1,0:T(8,128)S(1)}, u32[]{:S(2)}, u32[]{:S(2)}) collective-permute-start(f32[1,16,1024]{2,1,0:T(8,128)S(1)} %slice.182), channel_id=1, source_target_pairs={{16,0},{32,16},{48,32},{64,48},{80,64},{96,80},{112,96},{128,112},... | collective-permute-start | bytes 196616 | tf_op jit(solution)/shard_map/ppermute | solution.py:20
  633.7 14.4 %collective-permute-start.7 = (f32[8,1,1024]{2,1,0:T(1,128)S(1)}, f32[8,1,1024]{2,1,0:T(1,128)S(1)}, u32[]{:S(2)}, u32[]{:S(2)}) collective-permute-start(f32[8,1,1024]{2,1,0:T(1,128)S(1)} %slice.188), channel_id=1, source_target_pairs={{0,1},{1,2},{2,3},{3,4},{4,5},{5,6},{6,7},{7,8},{8,9},{9,10},{10,1... | collective-permute-start | bytes 98312 | tf_op jit(solution)/shard_map/ppermute | solution.py:20
  636.8 19.4 %collective-permute-start.6 = (f32[1,16,1024]{2,1,0:T(8,128)S(1)}, f32[1,16,1024]{2,1,0:T(8,128)S(1)}, u32[]{:S(2)}, u32[]{:S(2)}) collective-permute-start(f32[1,16,1024]{2,1,0:T(8,128)S(1)} %slice.186), channel_id=1, source_target_pairs={{0,16},{16,32},{32,48},{48,64},{64,80},{80,96},{96,112},{112,128},... | collective-permute-start | bytes 196616 | tf_op jit(solution)/shard_map/ppermute | solution.py:20
Sparse Core Ops, SparseCore 0:
  31.7 555.2 all-reduce.6
where the time goes:
time: 673 us
  waiting for transfers between devices  555 us (82%)
  starting transfers between devices  70.7 us (11%)
  other arithmetic  20.8 us (3%)
  between operations  20.5 us (3%)
    psum x1, waiting for transfers between devices, from_root(): return lax.psum(jnp.where(mine, value, jnp.zeros_like(value)), axis)  535 us
    ppermute x8, starting transfers between devices, passed_along(): lax.ppermute(value, axis, [(source, source + steps) for source in range(f...  70.7 us
    ppermute x8, waiting for transfers between devices, passed_along(): lax.ppermute(value, axis, [(source, source + steps) for source in range(f...  20.4 us
  transfers between devices with their start and end apart: 9, of which 3 were waited for; matrix products, arithmetic and copies ran while one was open for 1% of the time, Pallas kernels for 0%

commit v1 on v0

--- a/solution.py
+++ b/solution.py
@@ -7,11 +7,12 @@
 BINS = 8
 BAND = 6
 ITERS = 2
+pass_the_clusters = lambda vector, lane_axis: lax.all_gather(vector, lane_axis).sum(axis=0)
 
 
 def from_root(value, axis, root):
     mine = lax.axis_index(axis) == root
-    return lax.psum(jnp.where(mine, value, jnp.zeros_like(value)), axis)
+    return pass_the_clusters(jnp.where(mine, value, jnp.zeros_like(value)), axis)
 
 
 def passed_along(value, axis, steps):

time: 673 us -> 566 us (0.84)
  the two profiles are of different devices: /device:TPU:23 before, /device:TPU:67 now
where the time goes in v1:
time: 566 us
  waiting for transfers between devices  462 us (82%)
  starting transfers between devices  50 us (9%)
  other arithmetic  29.8 us (5%)
  between operations  20.5 us (4%)
    all_gather x2, waiting for transfers between devices, lax.all_gather(vector, lane_axis).sum(axis=0)  444 us
    ppermute x8, starting transfers between devices, passed_along(): lax.ppermute(value, axis, [(source, source + steps) for source in range(f...  49.9 us
    ppermute x8, waiting for transfers between devices, passed_along(): lax.ppermute(value, axis, [(source, source + steps) for source in range(f...  16.6 us
  transfers between devices with their start and end apart: 10, of which 4 were waited for; matrix products, arithmetic and copies ran while one was open for 3% of the time, Pallas kernels for 0%

profile of v1, /device:TPU:67, one launch (start us, length us, event | category | flops | bytes accessed | tf_op | source)
XLA Modules:
  0.0 565.6 jit_solution(10060643121510752463)
XLA Ops:
  7.2 0.0 copy-start
  7.2 0.0 copy-start.1
  7.2 0.0 all-gather.5.cloned.1.call-start
  7.2 1.3 fusion.28
  9.9 1.9 slice_select_fusion
  11.7 0.0 all-gather.5.cloned.1.call-update
  11.8 0.0 all-gather.7.cloned.1.call-start
  11.8 0.7 all-gather.7.cloned.1.call-update
  12.5 0.0 copy-done
  12.6 0.0 slice-start
  12.6 2.7 collective-permute-start.1
  15.3 16.1 %collective-permute-start = (f32[1,16,1024]{2,1,0:T(8,128)S(1)}, f32[1,16,1024]{2,1,0:T(8,128)S(1)}, u32[]{:S(2)}, u32[]{:S(2)}) collective-permute-start(f32[1,16,1024]{2,1,0:T(8,128)S(1)} %slice.131), channel_id=1, source_target_pairs={{16,0},{32,16},{48,32},{64,48},{80,64},{96,80},{112,96},{128,112},... | collective-permute-start | bytes 196616 | tf_op jit(solution)/shard_map/ppermute | solution.py:21
  31.4 0.0 copy-done.1
  31.4 0.7 fusion.27
  32.1 0.1 slice.133
  32.2 0.2 slice.136
  37.2 0.0 collective-permute-done.1
  37.2 1.5 collective-permute-done
  38.7 0.0 slice-done
  38.7 2.0 divide_select_fusion.3
  40.7 0.3 divide_select_fusion.5
  41.0 0.8 slice.173
  41.8 1.9 collective-permute-start.3
  43.8 10.1 %collective-permute-start.2 = (f32[1,16,1024]{2,1,0:T(8,128)S(1)}, f32[1,16,1024]{2,1,0:T(8,128)S(1)}, u32[]{:S(2)}, u32[]{:S(2)}) collective-permute-start(f32[1,16,1024]{2,1,0:T(8,128)S(1)} %slice.172), channel_id=1, source_target_pairs={{0,16},{16,32},{32,48},{48,64},{64,80},{80,96},{96,112},{112,128},... | collective-permute-start | bytes 196616 | tf_op jit(solution)/shard_map/ppermute | solution.py:21
  53.8 211.3 %all-gather.5.cloned.1.call-done = f32[32,1,4,16,1024]{4,3,2,1,0:T(8,128)} async-done(((f32[1,1,4,16,1024]{4,3,2,1,0:T(8,128)}), f32[32,1,4,16,1024]{4,3,2,1,0:T(8,128)}) %all-gather.5.cloned.1.call-update) | async-done | bytes 8388624 | tf_op jit(solution)/shard_map/all_gather | solution.py:10
  265.2 4.0 reduce_sum.18
  269.2 0.0 collective-permute-done.3
  269.2 0.0 collective-permute-done.2
  269.2 6.0 %multiply_subtract_fusion = (f32[8,16,1024]{2,1,0:T(8,128)S(1)}, f32[8,16,1024]{2,1,0:T(8,128)S(1)}) fusion(f32[8,16,1024]{2,1,0:T(8,128)S(1)} %copy-done, f32[]{:T(128)} %bitcast.11, f32[16,1024]{1,0:T(8,128)S(1)} %get-tuple-element.23, f32[]{:T(128)} %bitcast.9, f32[16,1024]{1,0:T(8,128)S(1)} %get-tuple-element.24, f32[]{:T(128)} %bitcast.7, ...), kind=kLoop, calls=%fused_computation.36 | loop fusion | flops 36831232 | bytes 4980272 | tf_op jit(solution)/shard_map/sub | solution.py:113
  275.2 3.0 collective-permute-start.5
  278.3 6.0 %collective-permute-start.4 = (f32[1,16,1024]{2,1,0:T(8,128)S(1)}, f32[1,16,1024]{2,1,0:T(8,128)S(1)}, u32[]{:S(2)}, u32[]{:S(2)}) collective-permute-start(f32[1,16,1024]{2,1,0:T(8,128)S(1)} %slice.182), channel_id=1, source_target_pairs={{16,0},{32,16},{48,32},{64,48},{80,64},{96,80},{112,96},{128,112},... | collective-permute-start | bytes 196616 | tf_op jit(solution)/shard_map/ppermute | solution.py:21
  284.2 233.1 %all-gather.7.cloned.1.call-done = f32[32,1,4,16,1024]{4,3,2,1,0:T(8,128)} async-done(((f32[1,1,4,16,1024]{4,3,2,1,0:T(8,128)}), f32[32,1,4,16,1024]{4,3,2,1,0:T(8,128)}) %all-gather.7.cloned.1.call-update) | async-done | bytes 8388624 | tf_op jit(solution)/shard_map/all_gather | solution.py:10
  517.4 4.0 reduce_sum.19
  521.4 0.2 slice.185
  521.6 0.1 slice.183
  521.7 0.0 collective-permute-done.5
  521.7 0.0 collective-permute-done.4
  521.7 0.6 divide_select_fusion
  522.3 0.2 divide_select_fusion.2
  522.6 8.3 %collective-permute-start.7 = (f32[8,1,1024]{2,1,0:T(1,128)S(1)}, f32[8,1,1024]{2,1,0:T(1,128)S(1)}, u32[]{:S(2)}, u32[]{:S(2)}) collective-permute-start(f32[8,1,1024]{2,1,0:T(1,128)S(1)} %slice.188), channel_id=1, source_target_pairs={{0,1},{1,2},{2,3},{3,4},{4,5},{5,6},{6,7},{7,8},{8,9},{9,10},{10,1... | collective-permute-start | bytes 98312 | tf_op jit(solution)/shard_map/ppermute | solution.py:21
  530.9 1.9 collective-permute-start.6
  532.8 1.2 pad_maximum_fusion
  534.1 0.0 collective-permute-done.7
  534.1 15.1 %collective-permute-done.6 = f32[1,16,1024]{2,1,0:T(8,128)S(1)} collective-permute-done((f32[1,16,1024]{2,1,0:T(8,128)S(1)}, f32[1,16,1024]{2,1,0:T(8,128)S(1)}, u32[]{:S(2)}, u32[]{:S(2)}) %collective-permute-start.6) | collective-permute-done | bytes 65568 | tf_op jit(solution)/shard_map/ppermute | solution.py:21
  549.2 9.6 %subtract_maximum_fusion = f32[8,16,1024]{2,1,0:T(8,128)} fusion(f32[8,16,1024]{2,1,0:T(8,128)S(1)} %get-tuple-element.7, f32[8,16,1024]{2,1,0:T(8,128)S(1)} %get-tuple-element.17, f32[8,15,1024]{2,1,0:T(8,128)S(1)} %bitcast.44, f32[8,1,1024]{2,1,0:T(1,128)S(1)} %collective-permute-done.7, f32[8,16,1024]{2,1,0:T(8,128)S(1)} %get-tuple-element.16, ...), kind=kLoop, calls=%fused_computation.30 | loop fusion | flops 65404928 | bytes 4718144 | tf_op jit(solution)/shard_map/max | solution.py:45
  (16 shorter events, 0.3 us)
Async XLA Ops:
  7.2 5.4 copy-start
  7.2 24.3 %copy-start.1 = (s32[2,4,1]{1,2,0:T(1,128)S(1)}, s32[2,4,1]{1,2,0:T(1,128)}, u32[]{:S(2)}) copy-start(s32[2,4,1]{1,2,0:T(1,128)} %param.9) | copy-start | bytes 100
  7.2 258.0 %all-gather.5.cloned.1.call-start = ((), (), s32[]{:S(2)}) async-start(), calls=%async_computation | async-start | bytes 8650752 | tf_op jit(solution)/shard_map/all_gather | solution.py:10
  11.8 505.6 %all-gather.7.cloned.1.call-start = ((), (), s32[]{:S(2)}) async-start(), calls=%async_computation.1 | async-start | bytes 8650752 | tf_op jit(solution)/shard_map/all_gather | solution.py:10
  12.6 26.1 %slice-start = ((f32[8,16,1024]{2,1,0:T(8,128)}), f32[7,16,1024]{2,1,0:T(8,128)S(1)}, s32[]{:S(2)}) async-start(f32[8,16,1024]{2,1,0:T(8,128)} %param.5), calls=%async_computation.2 | async-start | bytes 917504 | tf_op jit(solution)/shard_map/slice | solution.py:90
  12.6 24.6 %collective-permute-start.1 = (f32[8,1,1024]{2,1,0:T(1,128)S(1)}, f32[8,1,1024]{2,1,0:T(1,128)S(1)}, u32[]{:S(2)}, u32[]{:S(2)}) collective-permute-start(f32[8,1,1024]{2,1,0:T(1,128)S(1)} %slice.134), channel_id=1, source_target_pairs={{1,0},{2,1},{3,2},{4,3},{5,4},{6,5},{7,6},{8,7},{9,8},{10,9},{11,1... | collective-permute-start | bytes 98312 | tf_op jit(solution)/shard_map/ppermute | solution.py:21
  15.3 23.4 %collective-permute-start = (f32[1,16,1024]{2,1,0:T(8,128)S(1)}, f32[1,16,1024]{2,1,0:T(8,128)S(1)}, u32[]{:S(2)}, u32[]{:S(2)}) collective-permute-start(f32[1,16,1024]{2,1,0:T(8,128)S(1)} %slice.131), channel_id=1, source_target_pairs={{16,0},{32,16},{48,32},{64,48},{80,64},{96,80},{112,96},{128,112},... | collective-permute-start | bytes 196616 | tf_op jit(solution)/shard_map/ppermute | solution.py:21
  41.8 227.3 %collective-permute-start.3 = (f32[8,1,1024]{2,1,0:T(1,128)S(1)}, f32[8,1,1024]{2,1,0:T(1,128)S(1)}, u32[]{:S(2)}, u32[]{:S(2)}) collective-permute-start(f32[8,1,1024]{2,1,0:T(1,128)S(1)} %slice.174), channel_id=1, source_target_pairs={{0,1},{1,2},{2,3},{3,4},{4,5},{5,6},{6,7},{7,8},{8,9},{9,10},{10,1... | collective-permute-start | bytes 98312 | tf_op jit(solution)/shard_map/ppermute | solution.py:21
  43.8 225.4 %collective-permute-start.2 = (f32[1,16,1024]{2,1,0:T(8,128)S(1)}, f32[1,16,1024]{2,1,0:T(8,128)S(1)}, u32[]{:S(2)}, u32[]{:S(2)}) collective-permute-start(f32[1,16,1024]{2,1,0:T(8,128)S(1)} %slice.172), channel_id=1, source_target_pairs={{0,16},{16,32},{32,48},{48,64},{64,80},{80,96},{96,112},{112,128},... | collective-permute-start | bytes 196616 | tf_op jit(solution)/shard_map/ppermute | solution.py:21
  275.2 246.5 %collective-permute-start.5 = (f32[8,1,1024]{2,1,0:T(1,128)S(1)}, f32[8,1,1024]{2,1,0:T(1,128)S(1)}, u32[]{:S(2)}, u32[]{:S(2)}) collective-permute-start(f32[8,1,1024]{2,1,0:T(1,128)S(1)} %slice.184), channel_id=1, source_target_pairs={{1,0},{2,1},{3,2},{4,3},{5,4},{6,5},{7,6},{8,7},{9,8},{10,9},{11,1... | collective-permute-start | bytes 98312 | tf_op jit(solution)/shard_map/ppermute | solution.py:21
  278.3 243.4 %collective-permute-start.4 = (f32[1,16,1024]{2,1,0:T(8,128)S(1)}, f32[1,16,1024]{2,1,0:T(8,128)S(1)}, u32[]{:S(2)}, u32[]{:S(2)}) collective-permute-start(f32[1,16,1024]{2,1,0:T(8,128)S(1)} %slice.182), channel_id=1, source_target_pairs={{16,0},{32,16},{48,32},{64,48},{80,64},{96,80},{112,96},{128,112},... | collective-permute-start | bytes 196616 | tf_op jit(solution)/shard_map/ppermute | solution.py:21
  522.6 11.5 %collective-permute-start.7 = (f32[8,1,1024]{2,1,0:T(1,128)S(1)}, f32[8,1,1024]{2,1,0:T(1,128)S(1)}, u32[]{:S(2)}, u32[]{:S(2)}) collective-permute-start(f32[8,1,1024]{2,1,0:T(1,128)S(1)} %slice.188), channel_id=1, source_target_pairs={{0,1},{1,2},{2,3},{3,4},{4,5},{5,6},{6,7},{7,8},{8,9},{9,10},{10,1... | collective-permute-start | bytes 98312 | tf_op jit(solution)/shard_map/ppermute | solution.py:21
  530.9 18.3 %collective-permute-start.6 = (f32[1,16,1024]{2,1,0:T(8,128)S(1)}, f32[1,16,1024]{2,1,0:T(8,128)S(1)}, u32[]{:S(2)}, u32[]{:S(2)}) collective-permute-start(f32[1,16,1024]{2,1,0:T(8,128)S(1)} %slice.186), channel_id=1, source_target_pairs={{0,16},{16,32},{32,48},{48,64},{64,80},{80,96},{96,112},{112,128},... | collective-permute-start | bytes 196616 | tf_op jit(solution)/shard_map/ppermute | solution.py:21
Sparse Core Ops, SparseCore 0:
  12.3 252.7 all-gather.4
  270.0 247.2 all-gather.6
